TPU v7x, 32 devices: a whole 2x2x4 slice. The times are simulated.
32 devices in a mesh: dp: 2 (over core), ctx: 8 (over z, y), tp: 2 (over x).
Axes of the slice: x: 2, y: 2, z: 4, core: 2. Of those that a mesh axis runs over, the one named last changes fastest.
Arguments:
- prompt_states: bfloat16 [2048, 2048], P(('dp', 'ctx')), may hold values from -6 to 6
- continuation_states: bfloat16 [8192, 2048], P(('dp', 'ctx')), may hold values from -6 to 6
- continuation_offset: int32 [16], P(('dp', 'ctx')), may hold values from 0 to 511
- attention_gain: bfloat16 [2048], replicated, may hold values from 0.099609375 to 1.8984375
- query_weight: bfloat16 [2048, 1280], P(('dp', 'ctx'), 'tp'), may hold values from -0.125 to 0.125
- key_weight: bfloat16 [2048, 320], P(('dp', 'ctx')), may hold values from -0.125 to 0.125
- value_weight: bfloat16 [2048, 320], P(('dp', 'ctx')), may hold values from -0.125 to 0.125
- query_gain: bfloat16 [64], replicated, may hold values from 0.099609375 to 1.8984375
- key_gain: bfloat16 [64], replicated, may hold values from 0.099609375 to 1.8984375
- output_weight: bfloat16 [1280, 2048], P('tp', ('dp', 'ctx')), may hold values from -6 to 6
- feedforward_gain: bfloat16 [2048], replicated, may hold values from 0.099609375 to 1.8984375
- gate_weight: bfloat16 [2048, 5120], P(('dp', 'ctx'), 'tp'), may hold values from -0.125 to 0.125
- up_weight: bfloat16 [2048, 5120], P(('dp', 'ctx'), 'tp'), may hold values from -0.125 to 0.125
- down_weight: bfloat16 [5120, 2048], P('tp', ('dp', 'ctx')), may hold values from -0.078125 to 0.078125
- grad_prompt: bfloat16 [2048, 2048], P(('dp', 'ctx')), may hold values from -6 to 6
- grad_continuation: bfloat16 [8192, 2048], P(('dp', 'ctx')), may hold values from -6 to 6
Outputs:
- prompt_output: bfloat16 [2048, 2048], P(('dp', 'ctx'))
- continuation_output: bfloat16 [8192, 2048], P(('dp', 'ctx'))
- prompt_input_grad: bfloat16 [2048, 2048], P(('dp', 'ctx'))
- continuation_input_grad: bfloat16 [8192, 2048], P(('dp', 'ctx'))
- attention_gain_grad: float32 [2048], replicated
- query_weight_grad: float32 [2048, 1280], P(('dp', 'ctx'), 'tp')
- key_weight_grad: float32 [2048, 320], P(('dp', 'ctx'))
- value_weight_grad: float32 [2048, 320], P(('dp', 'ctx'))
- query_gain_grad: float32 [64], replicated
- key_gain_grad: float32 [64], replicated
- output_weight_grad: float32 [1280, 2048], P('tp', ('dp', 'ctx'))
- feedforward_gain_grad: float32 [2048], replicated
- gate_weight_grad: float32 [2048, 5120], P(('dp', 'ctx'), 'tp')
- up_weight_grad: float32 [2048, 5120], P(('dp', 'ctx'), 'tp')
- down_weight_grad: float32 [5120, 2048], P('tp', ('dp', 'ctx'))
All inputs are finite; a program needn't handle non-finite values.
Results may differ from a plain program's by a relative error of at most 0.019.
Values may be sent and summed in bfloat16 or wider, within the bound.
No kernel may reach another device: no remote copies, remote signals or barrier semaphores. Data moves between devices by JAX's collectives and lax.ppermute only.
A program may use at most 256 MiB of HBM per device.

v0:
```python
from functools import partial
import jax
import jax.numpy as jnp
from jax import lax
from jax.sharding import PartitionSpec as P

epsilon = 1e-06


def rms_norm(values, norm_gain):
    scale = lax.rsqrt(jnp.mean(values * values, axis=-1, keepdims=True) + epsilon)
    return values * scale * norm_gain


def rope_tables(positions, width):
    half_width = width // 2
    freqs = 10000.0 ** (-(2.0 * jnp.arange(half_width, dtype=jnp.float32)) / width)
    angles = positions[:, None] * freqs[None, :]
    angles = jnp.concatenate([angles, angles], axis=1)
    return (jnp.cos(angles), jnp.sin(angles))


def head_prep(raw_heads, norm_gain, cosine_table, sine_table):
    normed = rms_norm(raw_heads, norm_gain)
    half_width = raw_heads.shape[-1] // 2
    turned = jnp.concatenate([-normed[..., half_width:], normed[..., :half_width]], axis=-1)
    return normed * cosine_table[:, None, :] + turned * sine_table[:, None, :]


def swiglu(gate_rows, up_rows):
    return jax.nn.silu(gate_rows) * up_rows


def contract_last(left_rows, right_rows):
    return lax.dot_general(
        left_rows, right_rows, (((1,), (1,)), ((), ())), preferred_element_type=jnp.float32
    )


def contract_first(left_rows, right_rows):
    return lax.dot_general(
        left_rows, right_rows, (((0,), (0,)), ((), ())), preferred_element_type=jnp.float32
    )


def fold_columns(inputs, pieces):
    return tuple(
        (
            jnp.dot(inputs, weight_piece, preferred_element_type=jnp.float32)
            for weight_piece in pieces
        )
    )


def tensor_sum(values):
    return lax.psum(values.astype(jnp.bfloat16), "tp").astype(jnp.float32)


def on_device(
    prompt_states,
    continuation_states,
    continuation_offset,
    attention_gain,
    query_weight,
    key_weight,
    value_weight,
    query_gain,
    key_gain,
    output_weight,
    feedforward_gain,
    gate_weight,
    up_weight,
    down_weight,
    grad_prompt,
    grad_continuation,
):
    prompt_here = prompt_states.shape[0]
    cont_length = continuation_states.shape[0]
    rows_here = prompt_here + cont_length
    prompt_length = prompt_here * lax.axis_size("ctx")
    key_count = prompt_length + cont_length
    head_size = query_gain.shape[0]
    local_heads = query_weight.shape[1] // head_size
    shared_heads = key_weight.shape[1] // head_size
    group_size = local_heads * lax.axis_size("tp") // shared_heads
    context_rank = lax.axis_index("ctx")
    tensor_rank = lax.axis_index("tp")
    inputs = jnp.concatenate([prompt_states, continuation_states], axis=0)
    input_float = inputs.astype(jnp.float32)
    row_ids = jnp.arange(rows_here, dtype=jnp.int32)
    prompt_place = context_rank * prompt_here + row_ids
    positions = jnp.where(
        row_ids < prompt_here,
        prompt_place,
        prompt_length + continuation_offset[0] + row_ids - prompt_here,
    ).astype(jnp.float32)
    cosine_table, sine_table = rope_tables(positions, head_size)
    key_ids = jnp.arange(key_count, dtype=jnp.int32)
    allowed = jnp.where(
        (row_ids < prompt_here)[:, None],
        key_ids[None, :] <= prompt_place[:, None],
        (key_ids[None, :] < prompt_length)
        | (key_ids[None, :] - prompt_length <= (row_ids - prompt_here)[:, None]),
    )
    rotate = partial(head_prep, cosine_table=cosine_table, sine_table=sine_table)
    normed, attn_norm_back = jax.vjp(rms_norm, input_float, attention_gain.astype(jnp.float32))
    normed_low = normed.astype(jnp.bfloat16)
    query_raw, key_raw, value_raw = fold_columns(
        normed_low,
        (
            lax.all_gather(query_weight, ("dp", "ctx"), axis=0, tiled=True),
            lax.all_gather(key_weight, ("dp", "ctx"), axis=0, tiled=True),
            lax.all_gather(value_weight, ("dp", "ctx"), axis=0, tiled=True),
        ),
    )
    query_rot, query_back = jax.vjp(
        rotate, query_raw.reshape(rows_here, local_heads, head_size), query_gain.astype(jnp.float32)
    )
    query_low = query_rot.reshape(rows_here, local_heads * head_size).astype(jnp.bfloat16)
    key_rot, key_back = jax.vjp(
        rotate, key_raw.reshape(rows_here, shared_heads, head_size), key_gain.astype(jnp.float32)
    )
    key_low = key_rot.reshape(rows_here, shared_heads * head_size).astype(jnp.bfloat16)
    value_low = value_raw.astype(jnp.bfloat16)
    prompt_keys, prompt_values = (
        lax.all_gather(key_low[:prompt_here], "ctx", axis=0, tiled=True),
        lax.all_gather(value_low[:prompt_here], "ctx", axis=0, tiled=True),
    )
    all_keys = jnp.concatenate([prompt_keys, key_low[prompt_here:]], axis=0)
    all_values = jnp.concatenate([prompt_values, value_low[prompt_here:]], axis=0)

    def head_slices(head_index):
        shared_index = (tensor_rank * local_heads + head_index) // group_size
        query_head = lax.dynamic_slice_in_dim(query_low, head_index * head_size, head_size, 1)
        key_head = lax.dynamic_slice_in_dim(all_keys, shared_index * head_size, head_size, 1)
        value_head = lax.dynamic_slice_in_dim(all_values, shared_index * head_size, head_size, 1)
        return (query_head, key_head, value_head, shared_index)

    def scores_of(query_head, key_head):
        scores = contract_last(query_head, key_head) * 0.125
        return jnp.where(allowed, scores, -1e30)

    def head_forward(head_index):
        query_head, key_head, value_head, shared_index = head_slices(head_index)
        scores = scores_of(query_head, key_head)
        row_max = jnp.max(scores, axis=1, keepdims=True)
        weights = jnp.exp(scores - row_max)
        totals = jnp.sum(weights, axis=1, keepdims=True)
        probabilities = (weights / totals).astype(jnp.bfloat16)
        combined = jnp.dot(probabilities, value_head, preferred_element_type=jnp.float32)
        return (combined, (row_max + jnp.log(totals))[:, 0])

    per_head, log_sums = lax.map(head_forward, jnp.arange(local_heads, dtype=jnp.int32))
    attended_low = (
        jnp.transpose(per_head, (1, 0, 2))
        .reshape(rows_here, local_heads * head_size)
        .astype(jnp.bfloat16)
    )
    output_full, down_full = (
        lax.all_gather(output_weight, ("dp", "ctx"), axis=1, tiled=True),
        lax.all_gather(down_weight, ("dp", "ctx"), axis=1, tiled=True),
    )
    resid = input_float + tensor_sum(
        jnp.dot(attended_low, output_full, preferred_element_type=jnp.float32)
    )
    normed_two, ffn_norm_back = jax.vjp(rms_norm, resid, feedforward_gain.astype(jnp.float32))
    normed_two_low = normed_two.astype(jnp.bfloat16)
    gate_rows, up_rows = fold_columns(
        normed_two_low,
        (
            lax.all_gather(gate_weight, ("dp", "ctx"), axis=0, tiled=True),
            lax.all_gather(up_weight, ("dp", "ctx"), axis=0, tiled=True),
        ),
    )
    hidden, swiglu_back = jax.vjp(swiglu, gate_rows, up_rows)
    hidden_low = hidden.astype(jnp.bfloat16)
    output = resid + tensor_sum(jnp.dot(hidden_low, down_full, preferred_element_type=jnp.float32))
    prompt_output = output[:prompt_here].astype(jnp.bfloat16)
    continuation_output = output[prompt_here:].astype(jnp.bfloat16)
    grad_out = jnp.concatenate([grad_prompt, grad_continuation], axis=0)
    grad_down = contract_first(hidden_low, grad_out)
    output_back, down_back = (
        lax.all_gather(output_weight, ("dp", "ctx"), axis=1, tiled=True),
        lax.all_gather(down_weight, ("dp", "ctx"), axis=1, tiled=True),
    )
    grad_hidden = contract_last(grad_out, down_back)
    grad_gate, grad_up = swiglu_back(grad_hidden)
    grad_gate_low = grad_gate.astype(jnp.bfloat16)
    grad_up_low = grad_up.astype(jnp.bfloat16)
    grad_gate_weight = contract_first(normed_two_low, grad_gate_low)
    grad_up_weight = contract_first(normed_two_low, grad_up_low)
    pieces = (
        lax.all_gather(gate_weight, ("dp", "ctx"), axis=0, tiled=True),
        lax.all_gather(up_weight, ("dp", "ctx"), axis=0, tiled=True),
    )
    product = contract_last(grad_gate_low, pieces[0]) + contract_last(grad_up_low, pieces[1])
    grad_resid_part, grad_ffn_gain = ffn_norm_back(tensor_sum(product))
    grad_resid = grad_out.astype(jnp.float32) + grad_resid_part
    grad_resid_low = grad_resid.astype(jnp.bfloat16)
    grad_output_weight = contract_first(attended_low, grad_resid_low)
    grad_attended = contract_last(grad_resid_low, output_back).astype(jnp.bfloat16)

    def head_backward(carry, head_index):
        key_totals, value_totals = carry
        query_head, key_head, value_head, shared_index = head_slices(head_index)
        grad_head = lax.dynamic_slice_in_dim(grad_attended, head_index * head_size, head_size, 1)
        probabilities = jnp.exp(scores_of(query_head, key_head) - log_sums[head_index][:, None])
        grad_value = contract_first(probabilities.astype(jnp.bfloat16), grad_head)
        grad_probs = contract_last(grad_head, value_head)
        delta = jnp.sum(probabilities * grad_probs, axis=1, keepdims=True)
        grad_scores = (probabilities * (grad_probs - delta) * 0.125).astype(jnp.bfloat16)
        grad_query = jnp.dot(grad_scores, key_head, preferred_element_type=jnp.float32)
        grad_key = contract_first(grad_scores, query_head)
        column = shared_index * head_size
        key_totals = lax.dynamic_update_slice_in_dim(
            key_totals,
            lax.dynamic_slice_in_dim(key_totals, column, head_size, 1) + grad_key,
            column,
            1,
        )
        value_totals = lax.dynamic_update_slice_in_dim(
            value_totals,
            lax.dynamic_slice_in_dim(value_totals, column, head_size, 1) + grad_value,
            column,
            1,
        )
        return ((key_totals, value_totals), grad_query)

    zeros_keys = jnp.zeros((key_count, shared_heads * head_size), jnp.float32)
    (grad_keys, grad_values), grad_queries = lax.scan(
        head_backward, (zeros_keys, zeros_keys), jnp.arange(local_heads, dtype=jnp.int32)
    )
    grad_query_rot = jnp.transpose(grad_queries, (1, 0, 2))
    grad_query_raw, grad_query_gain = query_back(grad_query_rot)
    grad_query_low = grad_query_raw.reshape(rows_here, local_heads * head_size).astype(jnp.bfloat16)
    prompt_key_grad, prompt_value_grad = (
        lax.psum_scatter(
            grad_keys[:prompt_length].astype(jnp.bfloat16), "ctx", scatter_dimension=0, tiled=True
        ).astype(jnp.float32),
        lax.psum_scatter(
            grad_values[:prompt_length].astype(jnp.bfloat16), "ctx", scatter_dimension=0, tiled=True
        ).astype(jnp.float32),
    )
    own_key_grad = jnp.concatenate([prompt_key_grad, grad_keys[prompt_length:]], axis=0)
    own_value_grad = jnp.concatenate([prompt_value_grad, grad_values[prompt_length:]], axis=0)
    own_key_grad, own_value_grad, grad_query_gain = (
        lax.psum(own_key_grad.astype(jnp.bfloat16), "tp").astype(jnp.float32),
        lax.psum(own_value_grad.astype(jnp.bfloat16), "tp").astype(jnp.float32),
        lax.psum(grad_query_gain.astype(jnp.bfloat16), "tp").astype(jnp.float32),
    )
    grad_key_raw, grad_key_gain = key_back(own_key_grad.reshape(rows_here, shared_heads, head_size))
    grad_key_low = grad_key_raw.reshape(rows_here, shared_heads * head_size).astype(jnp.bfloat16)
    grad_value_low = own_value_grad.astype(jnp.bfloat16)
    grad_query_weight = contract_first(normed_low, grad_query_low)
    grad_key_weight = contract_first(normed_low, grad_key_low)
    grad_value_weight = contract_first(normed_low, grad_value_low)
    pieces = (
        lax.all_gather(query_weight, ("dp", "ctx"), axis=0, tiled=True),
        lax.all_gather(key_weight, ("dp", "ctx"), axis=0, tiled=True),
        lax.all_gather(value_weight, ("dp", "ctx"), axis=0, tiled=True),
    )
    query_part = contract_last(grad_query_low, pieces[0])
    shared_part = contract_last(grad_key_low, pieces[1]) + contract_last(grad_value_low, pieces[2])
    grad_normed = tensor_sum(query_part) + shared_part
    grad_input_part, grad_attn_gain = attn_norm_back(grad_normed)
    grad_input = (grad_resid + grad_input_part).astype(jnp.bfloat16)
    query_done, key_done, value_done, gate_done, up_done = (
        lax.psum_scatter(grad_query_weight, ("dp", "ctx"), scatter_dimension=0, tiled=True),
        lax.psum_scatter(grad_key_weight, ("dp", "ctx"), scatter_dimension=0, tiled=True),
        lax.psum_scatter(grad_value_weight, ("dp", "ctx"), scatter_dimension=0, tiled=True),
        lax.psum_scatter(grad_gate_weight, ("dp", "ctx"), scatter_dimension=0, tiled=True),
        lax.psum_scatter(grad_up_weight, ("dp", "ctx"), scatter_dimension=0, tiled=True),
    )
    outward = (
        lax.psum_scatter(grad_output_weight, ("dp", "ctx"), scatter_dimension=1, tiled=True),
        lax.psum_scatter(grad_down, ("dp", "ctx"), scatter_dimension=1, tiled=True),
    )
    gain_sums = lax.psum(
        (grad_attn_gain, grad_ffn_gain, grad_query_gain, grad_key_gain), ("dp", "ctx")
    )
    return (
        prompt_output,
        continuation_output,
        grad_input[:prompt_here],
        grad_input[prompt_here:],
        gain_sums[0],
        query_done,
        key_done,
        value_done,
        gain_sums[2],
        gain_sums[3],
        outward[0],
        gain_sums[1],
        gate_done,
        up_done,
        outward[1],
    )


def solution(mesh):
    in_specs = (
        P(("dp", "ctx"), None),
        P(("dp", "ctx"), None),
        P(("dp", "ctx")),
        P(),
        P(("dp", "ctx"), "tp"),
        P(("dp", "ctx"), None),
        P(("dp", "ctx"), None),
        P(),
        P(),
        P("tp", ("dp", "ctx")),
        P(),
        P(("dp", "ctx"), "tp"),
        P(("dp", "ctx"), "tp"),
        P("tp", ("dp", "ctx")),
        P(("dp", "ctx"), None),
        P(("dp", "ctx"), None),
    )
    out_specs = (
        P(("dp", "ctx"), None),
        P(("dp", "ctx"), None),
        P(("dp", "ctx"), None),
        P(("dp", "ctx"), None),
        P(),
        P(("dp", "ctx"), "tp"),
        P(("dp", "ctx"), None),
        P(("dp", "ctx"), None),
        P(),
        P(),
        P("tp", ("dp", "ctx")),
        P(),
        P(("dp", "ctx"), "tp"),
        P(("dp", "ctx"), "tp"),
        P("tp", ("dp", "ctx")),
    )
    return jax.shard_map(
        on_device, mesh=mesh, in_specs=in_specs, out_specs=out_specs, check_vma=False
    )
```

profile of v0, /device:TPU:0, one launch (start us, length us, event | category | flops | bytes accessed | tf_op | source)
XLA Modules:
  0.0 2214.9 jit_solution(14134863726572111871)
XLA Ops:
  17.5 33.2 %all-gather.10.cloned.1.call-done = bf16[2048,320]{0,1:T(8,128)(2,1)} async-done(((bf16[128,320]{0,1:T(8,128)(2,1)}), bf16[2048,320]{0,1:T(8,128)(2,1)}) %all-gather.10.cloned.1.call-update) | async-done | bytes 1310736 | tf_op jit(solution)/shard_map/all_gather | solution.py:112
  55.9 34.0 %all-gather.12.cloned.1.call-done = bf16[2048,320]{0,1:T(8,128)(2,1)} async-done(((bf16[128,320]{0,1:T(8,128)(2,1)}), bf16[2048,320]{0,1:T(8,128)(2,1)}) %all-gather.12.cloned.1.call-update) | async-done | bytes 1310736 | tf_op jit(solution)/shard_map/all_gather | solution.py:113
  94.0 30.2 %all_gather.36 = bf16[1024,320]{0,1:T(8,128)(2,1)S(1)} all-gather(bf16[128,320]{0,1:T(8,128)(2,1)S(1)} %slice.74), channel_id=1, replica_groups=mesh['dp'=2,'ctx'=8,'tp'=2] {'ctx'}, dimensions={0}, use_global_device_ids=true | all-gather | bytes 737280 | tf_op jit(solution)/shard_map/all_gather | solution.py:126
  127.5 29.9 %all_gather.38 = bf16[1024,320]{0,1:T(8,128)(2,1)S(1)} all-gather(bf16[128,320]{0,1:T(8,128)(2,1)S(1)} %slice.76), channel_id=1, replica_groups=mesh['dp'=2,'ctx'=8,'tp'=2] {'ctx'}, dimensions={0}, use_global_device_ids=true | all-gather | bytes 737280 | tf_op jit(solution)/shard_map/all_gather | solution.py:127
  160.8 4.8 fusion.73
  169.9 124.1 %while.34 = (s32[]{:T(128)}, bf16[10,640,64]{1,2,0:T(8,128)(2,1)}, f32[10,640]{1,0:T(8,128)}, s32[10]{0:T(128)S(1)}, bf16[640,640]{1,0:T(8,128)(2,1)S(1)}, /*ind...) while((s32[]{:T(128)}, bf16[10,640,64]{1,2,0:T(8,128)(2,1)}, ...), condition=%wide.region_6.7_spmd.clone.clone, body=%wide.region_3.6_spmd.clone.sunk.clone | while | flops 263454112 | bytes 28690356 | solution.py:153
  178.5 3.8 fusion.162
  191.0 3.8 fusion.162
  228.2 3.8 fusion.162
  240.6 3.8 fusion.162
  253.0 3.8 fusion.162
  265.4 3.8 fusion.162
  277.8 3.8 fusion.162
  294.1 5.8 convolution_convert_fusion.2
  307.4 65.5 %all-reduce.10.cloned.1.call-done = bf16[640,2048]{1,0:T(8,128)(2,1)} async-done(((bf16[640,2048]{1,0:T(8,128)(2,1)}), bf16[640,2048]{1,0:T(8,128)(2,1)}) %all-reduce.10.cloned.1.call-update) | async-done | bytes 2621456 | tf_op jit(solution)/shard_map/psum | solution.py:56
  378.7 84.5 %all-gather.16.cloned.1.call-done = bf16[2048,2560]{1,0:T(8,128)(2,1)} async-done(((bf16[128,2560]{1,0:T(8,128)(2,1)}), bf16[2048,2560]{1,0:T(8,128)(2,1)}) %all-gather.16.cloned.1.call-update) | async-done | bytes 10485776 | tf_op jit(solution)/shard_map/all_gather | solution.py:171
  463.1 12.3 fusion.75
  475.4 76.2 %all-gather.18.cloned.1.call-done = bf16[2048,2560]{1,0:T(8,128)(2,1)} async-done(((bf16[128,2560]{1,0:T(8,128)(2,1)}), bf16[2048,2560]{1,0:T(8,128)(2,1)}) %all-gather.18.cloned.1.call-update) | async-done | bytes 10485776 | tf_op jit(solution)/shard_map/all_gather | solution.py:172
  551.7 12.1 fusion.76
  563.8 79.1 %all-gather.20.cloned.1.call-done = bf16[2560,2048]{1,0:T(8,128)(2,1)} async-done(((bf16[2560,128]{1,0:T(8,128)(2,1)}), bf16[2560,2048]{1,0:T(8,128)(2,1)}) %all-gather.20.cloned.1.call-update) | async-done | bytes 10485776 | tf_op jit(solution)/shard_map/all_gather | solution.py:161
  642.9 17.8 multiply_convert_fusion.1
  660.8 10.8 fusion.77
  671.6 11.0 add_convert_fusion
  682.7 72.6 %all-reduce.12.cloned.1.call-done = bf16[640,2048]{1,0:T(8,128)(2,1)} async-done(((bf16[640,2048]{1,0:T(8,128)(2,1)}), bf16[640,2048]{1,0:T(8,128)(2,1)}) %all-reduce.12.cloned.1.call-update) | async-done | bytes 2621456 | tf_op jit(solution)/shard_map/psum | solution.py:56
  755.3 4.7 fusion.43
  760.2 6.2 convolution_convert_fusion.3
  769.4 208.5 %while.35 = (s32[]{:T(128)}, f32[1536,320]{0,1:T(8,128)}, f32[1536,320]{0,1:T(8,128)}, f32[10,640,64]{1,2,0:T(8,128)}, s32[10]{0:T(128)S(1)}, /*index=5*/s32[]{:...) while((s32[]{:T(128)}, f32[1536,320]{0,1:T(8,128)}, ...), condition=%wide.region_14.15_spmd.clone.clone, body=%wide.region_12.14_spmd.clone.sunk.clone | while | flops 643104128 | bytes 48826372 | solution.py:230
  777.8 4.7 multiply_reduce_fusion.10
  792.2 3.8 fusion.171
  798.7 4.7 multiply_reduce_fusion.10
  813.0 3.8 fusion.171
  819.5 4.7 multiply_reduce_fusion.10
  833.9 3.8 fusion.171
  840.4 4.7 multiply_reduce_fusion.10
  861.2 4.7 multiply_reduce_fusion.10
  875.6 3.8 fusion.171
  882.1 4.7 multiply_reduce_fusion.10
  896.4 3.8 fusion.171
  902.9 4.7 multiply_reduce_fusion.10
  917.3 3.8 fusion.171
  923.8 4.7 multiply_reduce_fusion.10
  938.1 3.8 fusion.171
  944.6 4.7 multiply_reduce_fusion.10
  959.0 3.8 fusion.171
  965.5 4.7 multiply_reduce_fusion.10
  981.8 12.3 convolution_convert_fusion.1
  1008.4 36.1 %reduce-scatter.30.cloned.1.call-done = bf16[128,320]{1,0:T(8,128)(2,1)} async-done(((bf16[1024,320]{1,0:T(8,128)(2,1)}), bf16[128,320]{1,0:T(8,128)(2,1)}) %reduce-scatter.30.cloned.1.call-update) | async-done | bytes 81936
  1046.2 63.9 %reduce-scatter.28.cloned.1.call-done = bf16[128,320]{1,0:T(8,128)(2,1)} async-done(((bf16[1024,320]{1,0:T(8,128)(2,1)}), bf16[128,320]{1,0:T(8,128)(2,1)}) %reduce-scatter.28.cloned.1.call-update) | async-done | bytes 81936
  1113.1 8.2 fusion.53
  1122.5 6.6 fusion.79
  1129.4 132.1 %all-reduce.14.cloned.1.call-done = (bf16[640,2048]{1,0:T(8,128)(2,1)}, bf16[640,5,64]{0,2,1:T(8,128)(2,1)}, bf16[640,2048]{1,0:T(8,128)(2,1)}, bf16[640,320]{0,1:T(8,128)(2,1)}) async-done(((bf16[640,2048]{1,0:T(8,128)(2,1)}, bf16[640,5,64]{0,2,1:T(8,128)(2,1)}, bf16[640,2048]{1,0:T(8,128)(2,1)}, bf16[640,320]{0,1:T(8,128)(2,1)}), (bf16[640,2048]{1,0:T(8,128)(2,1)}, bf16[640,5,64]{0,2,1:T(8,128)(2,1)}, ...) | async-done | bytes 6062096 | tf_op jit(solution)/shard_map/psum | solution.py:56
  1268.3 4.4 fusion.84
  1272.8 15.2 fusion.80
  1288.1 14.9 fusion.81
  1303.3 14.7 fusion.82
  1318.0 5.1 psum.84
  1329.6 6.9 fusion.46
  1341.1 61.1 %all-reduce.4 = (f32[2048]{0:T(1024)}, f32[64]{0:T(128)}, f32[64]{0:T(128)}, f32[2048]{0:T(1024)}) all-reduce(f32[2048]{0:T(1024)S(1)} %get-tuple-element.423, bf16[64]{0:T(256)(128)(2,1)S(1)} %psum.84, f32[64]{0:T(128)S(1)} %get-tuple-element.427, f32[2048]{0:T(1024)S(1)} %copy-done.46), channel_id=1, replica_groups=mesh['dp'=2,'ctx'=8,'tp'=2] {'dp','ctx'}, use_global_device_ids=true, to_apply=%region_24.25 | all-reduce | flops 4224 | bytes 33664 | tf_op jit(solution)/shard_map/psum | solution.py:278
  1402.2 25.7 %reduce-scatter.14.cloned.1.call-done = f32[128,640]{1,0:T(8,128)} async-done(((f32[2048,640]{1,0:T(8,128)}), f32[128,640]{1,0:T(8,128)}) %reduce-scatter.14.cloned.1.call-update) | async-done | bytes 327696 | tf_op jit(solution)/shard_map/reduce_scatter | solution.py:268
  1427.9 67.5 %reduce-scatter.16.cloned.1.call-done = f32[128,320]{0,1:T(8,128)} async-done(((f32[2048,320]{0,1:T(8,128)}), f32[128,320]{0,1:T(8,128)}) %reduce-scatter.16.cloned.1.call-update) | async-done | bytes 163856 | tf_op jit(solution)/shard_map/reduce_scatter | solution.py:269
  1495.4 67.6 %reduce-scatter.18.cloned.1.call-done = f32[128,320]{0,1:T(8,128)} async-done(((f32[2048,320]{0,1:T(8,128)}), f32[128,320]{0,1:T(8,128)}) %reduce-scatter.18.cloned.1.call-update) | async-done | bytes 163856 | tf_op jit(solution)/shard_map/reduce_scatter | solution.py:270
  1563.0 215.0 %reduce-scatter.22.cloned.1.call-done = f32[128,2560]{1,0:T(8,128)} async-done(((f32[2048,2560]{1,0:T(8,128)}), f32[128,2560]{1,0:T(8,128)}) %reduce-scatter.22.cloned.1.call-update) | async-done | bytes 1310736 | tf_op jit(solution)/shard_map/reduce_scatter | solution.py:271
  1778.0 215.1 %reduce-scatter.24.cloned.1.call-done = f32[128,2560]{1,0:T(8,128)} async-done(((f32[2048,2560]{1,0:T(8,128)}), f32[128,2560]{1,0:T(8,128)}) %reduce-scatter.24.cloned.1.call-update) | async-done | bytes 1310736 | tf_op jit(solution)/shard_map/reduce_scatter | solution.py:272
  1993.1 215.1 %reduce-scatter.26.cloned.1.call-done = f32[2560,128]{1,0:T(8,128)} async-done(((f32[2560,2048]{1,0:T(8,128)}), f32[2560,128]{1,0:T(8,128)}) %reduce-scatter.26.cloned.1.call-update) | async-done | bytes 1310736 | tf_op jit(solution)/shard_map/reduce_scatter | solution.py:276
  (410 shorter events, 269.7 us)
Async XLA Ops:
  7.2 8.1 copy-start.11
  7.2 8.1 copy-start.2
  7.2 6.8 copy-start.51
  7.2 6.8 copy-start.53
  7.2 8.0 copy-start.54
  7.2 43.4 %all-gather.10.cloned.1.call-start = ((), (), s32[]{:S(2)}) async-start(), calls=%async_computation.10 | async-start | bytes 1392640 | tf_op jit(solution)/shard_map/all_gather | solution.py:112
  8.0 81.9 %all-gather.12.cloned.1.call-start = ((), (), s32[]{:S(2)}) async-start(), calls=%async_computation.11 | async-start | bytes 1392640 | tf_op jit(solution)/shard_map/all_gather | solution.py:113
  8.7 152.1 %all-gather.8.cloned.1.call-start = ((), (), s32[]{:S(2)}) async-start(), calls=%async_computation.9 | async-start | bytes 2785280 | tf_op jit(solution)/shard_map/all_gather | solution.py:111
  9.5 284.6 %all-gather.14.cloned.1.call-start = ((), (), s32[]{:S(2)}) async-start(), calls=%async_computation.12 | async-start | bytes 2785280 | tf_op jit(solution)/shard_map/all_gather | solution.py:160
  10.0 362.9 %all-reduce.10.cloned.1.call-start = ((), (), s32[]{:S(2)}) async-start(), calls=%async_computation.13 | async-start | bytes 5242880 | tf_op jit(solution)/shard_map/psum | solution.py:56
  14.0 3.5 copy-start.44
  14.0 3.5 copy-start.40
  14.0 40.1 %copy-start.47 = (f32[64]{0:T(128)}, f32[64]{0:T(128)S(1)}, u32[]{:S(2)}) copy-start(f32[64]{0:T(128)S(1)} %convert_element_type.144) | copy-start | bytes 772
  15.1 151.6 %copy-start.20 = (f32[640,64]{0,1:T(8,128)}, f32[640,64]{0,1:T(8,128)S(1)}, u32[]{:S(2)}) copy-start(f32[640,64]{0,1:T(8,128)S(1)} %get-tuple-element.514) | copy-start | bytes 491524
  15.1 151.7 %copy-start.15 = (f32[640,64]{0,1:T(8,128)}, f32[640,64]{0,1:T(8,128)S(1)}, u32[]{:S(2)}) copy-start(f32[640,64]{0,1:T(8,128)S(1)} %get-tuple-element.513) | copy-start | bytes 491524
  15.2 150.6 %copy-start.49 = (f32[64]{0:T(128)}, f32[64]{0:T(128)S(1)}, u32[]{:S(2)}) copy-start(f32[64]{0:T(128)S(1)} %convert_element_type.141) | copy-start | bytes 772
  55.9 68.3 %copy-start.26 = (bf16[512,320]{0,1:T(8,128)(2,1)S(1)}, bf16[512,320]{0,1:T(8,128)(2,1)}, u32[]{:S(2)}) copy-start(bf16[512,320]{0,1:T(8,128)(2,1)} %slice.75) | copy-start | bytes 983044
  125.2 32.3 %copy-start.27 = (bf16[512,320]{0,1:T(8,128)(2,1)S(1)}, bf16[512,320]{0,1:T(8,128)(2,1)}, u32[]{:S(2)}) copy-start(bf16[512,320]{0,1:T(8,128)(2,1)} %slice.77) | copy-start | bytes 983044
  299.8 163.3 %all-gather.16.cloned.1.call-start = ((), (), s32[]{:S(2)}) async-start(), calls=%async_computation.14 | async-start | bytes 11141120 | tf_op jit(solution)/shard_map/all_gather | solution.py:171
  300.4 251.3 %all-gather.18.cloned.1.call-start = ((), (), s32[]{:S(2)}) async-start(), calls=%async_computation.15 | async-start | bytes 11141120 | tf_op jit(solution)/shard_map/all_gather | solution.py:172
  301.2 341.8 %all-gather.20.cloned.1.call-start = ((), (), s32[]{:S(2)}) async-start(), calls=%async_computation.16 | async-start | bytes 11141120 | tf_op jit(solution)/shard_map/all_gather | solution.py:161
  301.9 453.4 %all-reduce.12.cloned.1.call-start = ((), (), s32[]{:S(2)}) async-start(), calls=%async_computation.17 | async-start | bytes 5242880 | tf_op jit(solution)/shard_map/psum | solution.py:56
  372.9 2.8 copy-start.3
  660.8 10.8 copy-start.59
  682.6 361.8 %reduce-scatter.30.cloned.1.call-start = ((), (), s32[]{:S(2)}) async-start(), calls=%async_computation.26 | async-start | bytes 884736
  755.3 4.8 copy-start.4
  755.3 4.8 copy-start.13
  755.3 4.9 copy-start.56
  777.8 4.7 copy-start
  798.7 4.7 copy-start
  819.5 4.7 copy-start
  840.4 4.7 copy-start
  861.2 4.7 copy-start
  882.1 4.7 copy-start
  902.9 4.7 copy-start
  923.8 4.7 copy-start
  944.6 4.7 copy-start
  965.5 4.7 copy-start
  981.8 128.4 %reduce-scatter.28.cloned.1.call-start = ((), (), s32[]{:S(2)}) async-start(), calls=%async_computation.25 | async-start | bytes 884736
  981.8 12.3 copy-start.12
  999.2 262.3 %all-reduce.14.cloned.1.call-start = ((), (), s32[]{:S(2)}) async-start(), calls=%async_computation.27 | async-start | bytes 12124160 | tf_op jit(solution)/shard_map/psum | solution.py:56
  999.3 3.3 copy-start.37
  999.3 3.3 copy-start.7
  1004.6 40.8 %slice-start = ((bf16[1536,320]{0,1:T(8,128)(2,1)}), bf16[512,320]{0,1:T(8,128)(2,1)S(1)}, s32[]{:S(2)}) async-start(bf16[1536,320]{0,1:T(8,128)(2,1)} %copy-done.22), calls=%async_computation.28 | async-start | bytes 655360 | tf_op jit(solution)/shard_map/slice | solution.py:245
  1004.6 106.6 %slice-start.1 = ((bf16[1536,320]{0,1:T(8,128)(2,1)}), bf16[512,320]{0,1:T(8,128)(2,1)S(1)}, s32[]{:S(2)}) async-start(bf16[1536,320]{0,1:T(8,128)(2,1)} %copy-done.23), calls=%async_computation.29 | async-start | bytes 655360 | tf_op jit(solution)/shard_map/slice | solution.py:244
  1112.0 290.2 %reduce-scatter.20.cloned.1.call-start = ((), (), s32[]{:S(2)}) async-start(), calls=%async_computation.21 | async-start | bytes 5570560 | tf_op jit(solution)/shard_map/reduce_scatter | solution.py:275
  1121.4 306.5 %reduce-scatter.14.cloned.1.call-start = ((), (), s32[]{:S(2)}) async-start(), calls=%async_computation.18 | async-start | bytes 5570560 | tf_op jit(solution)/shard_map/reduce_scatter | solution.py:268
  1129.2 133.6 %copy-start.10 = (f32[640,320]{0,1:T(8,128)S(1)}, f32[640,320]{0,1:T(8,128)}, u32[]{:S(2)}) copy-start(f32[640,320]{0,1:T(8,128)} %copy-done.9) | copy-start | bytes 2457604
  1129.2 133.6 %copy-start.35 = (f32[640,5]{0,1:T(8,128)S(1)}, f32[640,5]{0,1:T(8,128)}, u32[]{:S(2)}) copy-start(f32[640,5]{0,1:T(8,128)} %copy-done.34) | copy-start | bytes 38404
  1129.2 133.6 %copy-start.48 = (f32[64]{0:T(128)S(1)}, f32[64]{0:T(128)}, u32[]{:S(2)}) copy-start(f32[64]{0:T(128)} %copy-done.47) | copy-start | bytes 772
  1129.2 366.2 %reduce-scatter.16.cloned.1.call-start = ((), (), s32[]{:S(2)}) async-start(), calls=%async_computation.19 | async-start | bytes 2785280 | tf_op jit(solution)/shard_map/reduce_scatter | solution.py:269
  1267.3 295.7 %reduce-scatter.18.cloned.1.call-start = ((), (), s32[]{:S(2)}) async-start(), calls=%async_computation.20 | async-start | bytes 2785280 | tf_op jit(solution)/shard_map/reduce_scatter | solution.py:270
  1272.8 505.2 %reduce-scatter.22.cloned.1.call-start = ((), (), s32[]{:S(2)}) async-start(), calls=%async_computation.22 | async-start | bytes 22282240 | tf_op jit(solution)/shard_map/reduce_scatter | solution.py:271
  1288.0 705.0 %reduce-scatter.24.cloned.1.call-start = ((), (), s32[]{:S(2)}) async-start(), calls=%async_computation.23 | async-start | bytes 22282240 | tf_op jit(solution)/shard_map/reduce_scatter | solution.py:272
  1303.0 905.1 %reduce-scatter.26.cloned.1.call-start = ((), (), s32[]{:S(2)}) async-start(), calls=%async_computation.24 | async-start | bytes 22282240 | tf_op jit(solution)/shard_map/reduce_scatter | solution.py:276
  1318.0 5.1 copy-start.19
  1323.1 3.1 copy-start.41
  1323.1 3.1 copy-start.45
  1323.1 3.1 copy-start.57
  1323.1 3.1 copy-start.58
  1326.2 3.2 copy-start.43
  1326.2 3.3 copy-start.5
  1326.2 3.3 copy-start.14
  1326.3 3.3 copy-start.25
  (35 other events, 51.2 us)
Sparse Core Ops, SparseCore 0:
  10.1 40.4 all-gather.9
  52.7 37.0 all-gather.11
  92.1 45.4 all-gather.7
  139.5 45.6 all-gather.13
  300.0 72.8 all-reduce.9
  375.2 87.8 all-gather.15
  465.6 86.0 all-gather.17
  554.0 88.9 all-gather.19
  682.7 72.5 all-reduce.11
  981.9 62.4 reduce-scatter.29
  1048.7 61.4 reduce-scatter.27
  1113.2 148.2 all-reduce.13
  1266.5 78.7 reduce-scatter.19
  1350.1 77.7 reduce-scatter.13
  1432.6 62.8 reduce-scatter.15
  1500.1 62.8 reduce-scatter.17
  1568.1 209.8 reduce-scatter.21
  1783.1 209.9 reduce-scatter.23
  1998.3 209.7 reduce-scatter.25
where the time goes:
time: 2220 us; the launch traced here: 2210 us
  waiting for transfers between devices  1490 us (67%)
  matrix products  399 us (18%)
  blocking collectives  126 us (6%)
  local copies, waits for them, and re-layouts  86.6 us (4%)
  other arithmetic  51.4 us (2%)
  loops' own time  46.6 us (2%)
    psum x3, waiting for transfers between devices, tensor_sum(): return lax.psum(values.astype(jnp.bfloat16), 'tp').astype(jnp.float32)  270 us
    reduce_scatter x1, waiting for transfers between devices, on_device(): lax.psum_scatter(grad_up_weight, ('dp', 'ctx'), scatter_dimension=0, tile...  215 us
    reduce_scatter x1, waiting for transfers between devices, on_device(): lax.psum_scatter(grad_down, ('dp', 'ctx'), scatter_dimension=1, tiled=True)  215 us
    reduce_scatter x1, waiting for transfers between devices, on_device(): lax.psum_scatter(grad_gate_weight, ('dp', 'ctx'), scatter_dimension=0, ti...  215 us
    dot_general x37, matrix products, contract_last(): lax.dot_general(left_rows, right_rows, (((1,), (1,)), ((), ())), preferre...  169 us
    dot_general x27, matrix products, contract_first(): lax.dot_general(left_rows, right_rows, (((0,), (0,)), ((), ())), preferre...  114 us
    unnamed x21, waiting for transfers between devices  105 us
    all_gather x1, waiting for transfers between devices, on_device(): lax.all_gather(gate_weight, ('dp', 'ctx'), axis=0, tiled=True)  84.5 us
  transfers between devices with their start and end apart: 19, of which 16 were waited for; matrix products, arithmetic and copies ran while one was open for 12% of the time, Pallas kernels for 0%

commit v1 on v0

--- a/solution.py
+++ b/solution.py
@@ -74,6 +74,32 @@
     grad_prompt,
     grad_continuation,
 ):
+
+    def list_plate(field, pos_dim):
+        k_now = lax.axis_size(("dp", "ctx"))
+        near, high, value_now = (k_now, lax.axis_index(("dp", "ctx")), field.shape[pos_dim])
+        heard = tuple((p * near if no == pos_dim else p for no, p in enumerate(field.shape)))
+        reply = jnp.zeros(heard, field.dtype)
+        outer = lax.dynamic_update_slice_in_dim(reply, field, high * value_now, axis=pos_dim)
+        z = block_now = field
+        for hop_no in range(1, near // 2 + 1):
+            z = lax.ppermute(
+                z, ("dp", "ctx"), perm=tuple(((no, (no + 1) % near) for no in range(near)))
+            )
+            outer = lax.dynamic_update_slice_in_dim(
+                outer, z, (high - hop_no) % near * value_now, axis=pos_dim
+            )
+            if 2 * hop_no < near:
+                block_now = lax.ppermute(
+                    block_now,
+                    axis_name=("dp", "ctx"),
+                    perm=tuple(((no, (no - 1) % near) for no in range(near))),
+                )
+                outer = lax.dynamic_update_slice_in_dim(
+                    outer, block_now, (high + hop_no) % near * value_now, axis=pos_dim
+                )
+        return outer
+
     prompt_here = prompt_states.shape[0]
     cont_length = continuation_states.shape[0]
     rows_here = prompt_here + cont_length
@@ -167,10 +193,7 @@
     normed_two_low = normed_two.astype(jnp.bfloat16)
     gate_rows, up_rows = fold_columns(
         normed_two_low,
-        (
-            lax.all_gather(gate_weight, ("dp", "ctx"), axis=0, tiled=True),
-            lax.all_gather(up_weight, ("dp", "ctx"), axis=0, tiled=True),
-        ),
+        (lax.all_gather(gate_weight, ("dp", "ctx"), axis=0, tiled=True), list_plate(up_weight, 0)),
     )
     hidden, swiglu_back = jax.vjp(swiglu, gate_rows, up_rows)
     hidden_low = hidden.astype(jnp.bfloat16)

time: 2220 us -> 2280 us (1.027)
  starting transfers between devices: 1.15 us -> 71.7 us
  waiting for transfers between devices: 1490 us -> 1450 us
  local copies, waits for them, and re-layouts: 86.6 us -> 110 us
    ppermute x0 -> x15, waiting for transfers between devices: none -> 157 us  [the longest x8 156 us: list_plate(): lax.ppermute(z, ('dp', 'ctx'), perm=tuple(((no, (no + 1) % near) for no i...]
    all_gather x1, waiting for transfers between devices: 84.5 us -> 0.01 us  [on_device(): lax.all_gather(gate_weight, ('dp', 'ctx'), axis=0, tiled=True)]
    ppermute x0 -> x15, starting transfers between devices: none -> 70.4 us  [the longest x7 55.4 us: list_plate(): lax.ppermute(block_now, axis_name=('dp', 'ctx'), perm=tuple(((no, (no - 1...]
    psum x3, waiting for transfers between devices: 270 us -> 205 us  [tensor_sum(): return lax.psum(values.astype(jnp.bfloat16), 'tp').astype(jnp.float32)]
    all_gather x1, waiting for transfers between devices: 76.2 us -> 46.6 us  [on_device(): lax.all_gather(up_weight, ('dp', 'ctx'), axis=0, tiled=True)]
  transfers between devices with their start and end apart: 19 -> 34, of which waited for: 16 -> 23; matrix products, arithmetic and copies ran while one was open for 12% -> 14% of each run, Pallas kernels for 0% -> 0%
where the time goes in v1:
time: 2280 us; the launch traced here: 2270 us
  waiting for transfers between devices  1450 us (64%)
  matrix products  401 us (18%)
  blocking collectives  126 us (6%)
  local copies, waits for them, and re-layouts  110 us (5%)
  starting transfers between devices  71.7 us (3%)
  other arithmetic  52.5 us (2%)
  loops' own time  46.6 us (2%)
    reduce_scatter x1, waiting for transfers between devices, on_device(): lax.psum_scatter(grad_down, ('dp', 'ctx'), scatter_dimension=1, tiled=True)  215 us
    reduce_scatter x1, waiting for transfers between devices, on_device(): lax.psum_scatter(grad_up_weight, ('dp', 'ctx'), scatter_dimension=0, tile...  215 us
    reduce_scatter x1, waiting for transfers between devices, on_device(): lax.psum_scatter(grad_gate_weight, ('dp', 'ctx'), scatter_dimension=0, ti...  215 us
    psum x3, waiting for transfers between devices, tensor_sum(): return lax.psum(values.astype(jnp.bfloat16), 'tp').astype(jnp.float32)  205 us
    dot_general x37, matrix products, contract_last(): lax.dot_general(left_rows, right_rows, (((1,), (1,)), ((), ())), preferre...  166 us
    ppermute x8, waiting for transfers between devices, list_plate(): lax.ppermute(z, ('dp', 'ctx'), perm=tuple(((no, (no + 1) % near) for no i...  156 us
    dot_general x27, matrix products, contract_first(): lax.dot_general(left_rows, right_rows, (((0,), (0,)), ((), ())), preferre...  114 us
    unnamed x21, waiting for transfers between devices  103 us
  transfers between devices with their start and end apart: 34, of which 23 were waited for; matrix products, arithmetic and copies ran while one was open for 14% of the time, Pallas kernels for 0%

profile of v1, /device:TPU:0, one launch (start us, length us, event | category | flops | bytes accessed | tf_op | source)
XLA Modules:
  0.0 2273.6 jit_solution(1551617717853152149)
XLA Ops:
  17.5 33.1 %all-gather.10.cloned.1.call-done = bf16[2048,320]{0,1:T(8,128)(2,1)} async-done(((bf16[128,320]{0,1:T(8,128)(2,1)}), bf16[2048,320]{0,1:T(8,128)(2,1)}) %all-gather.10.cloned.1.call-update) | async-done | bytes 1310736 | tf_op jit(solution)/shard_map/all_gather | solution.py:138
  55.7 34.2 %all-gather.12.cloned.1.call-done = bf16[2048,320]{0,1:T(8,128)(2,1)} async-done(((bf16[128,320]{0,1:T(8,128)(2,1)}), bf16[2048,320]{0,1:T(8,128)(2,1)}) %all-gather.12.cloned.1.call-update) | async-done | bytes 1310736 | tf_op jit(solution)/shard_map/all_gather | solution.py:139
  94.0 30.3 %all_gather.35 = bf16[1024,320]{0,1:T(8,128)(2,1)S(1)} all-gather(bf16[128,320]{0,1:T(8,128)(2,1)S(1)} %slice.74), channel_id=1, replica_groups=mesh['dp'=2,'ctx'=8,'tp'=2] {'ctx'}, dimensions={0}, use_global_device_ids=true | all-gather | bytes 737280 | tf_op jit(solution)/shard_map/all_gather | solution.py:152
  127.6 29.9 %all_gather.37 = bf16[1024,320]{0,1:T(8,128)(2,1)S(1)} all-gather(bf16[128,320]{0,1:T(8,128)(2,1)S(1)} %slice.76), channel_id=1, replica_groups=mesh['dp'=2,'ctx'=8,'tp'=2] {'ctx'}, dimensions={0}, use_global_device_ids=true | all-gather | bytes 737280 | tf_op jit(solution)/shard_map/all_gather | solution.py:153
  161.8 4.8 fusion.73
  170.9 124.1 %while.34 = (s32[]{:T(128)}, bf16[10,640,64]{1,2,0:T(8,128)(2,1)}, f32[10,640]{1,0:T(8,128)}, s32[10]{0:T(128)S(1)}, bf16[640,640]{1,0:T(8,128)(2,1)S(1)}, /*ind...) while((s32[]{:T(128)}, bf16[10,640,64]{1,2,0:T(8,128)(2,1)}, ...), condition=%wide.region_6.7_spmd.clone.clone, body=%wide.region_3.6_spmd.clone.sunk.clone | while | flops 263454112 | bytes 28690356 | solution.py:179
  179.6 3.8 fusion.162
  295.1 5.8 convolution_convert_fusion.2
  303.1 4.5 collective-permute-start.1
  312.6 4.6 broadcast_in_dim.82
  318.1 5.4 collective-permute-done
  327.0 8.1 collective-permute-start.3
  339.1 13.3 collective-permute-done.2
  354.8 8.4 collective-permute-start.5
  365.0 17.1 collective-permute-done.4
  384.8 9.5 collective-permute-start.7
  396.1 23.0 %collective-permute-done.6 = bf16[128,2560]{1,0:T(8,128)(2,1)S(1)} collective-permute-done((bf16[128,2560]{1,0:T(8,128)(2,1)S(1)}, bf16[128,2560]{1,0:T(8,128)(2,1)S(1)}, u32[]{:S(2)}, u32[]{:S(2)}) %collective-permute-start.6) | collective-permute-done | bytes 655392 | tf_op jit(solution)/shard_map/ppermute | solution.py:86
  421.6 4.7 collective-permute-start.9
  428.1 35.6 %collective-permute-done.8 = bf16[128,2560]{1,0:T(8,128)(2,1)S(1)} collective-permute-done((bf16[128,2560]{1,0:T(8,128)(2,1)S(1)}, bf16[128,2560]{1,0:T(8,128)(2,1)S(1)}, u32[]{:S(2)}, u32[]{:S(2)}) %collective-permute-start.8) | collective-permute-done | bytes 655392 | tf_op jit(solution)/shard_map/ppermute | solution.py:86
  466.1 10.1 collective-permute-start.11
  478.0 27.6 %collective-permute-done.10 = bf16[128,2560]{1,0:T(8,128)(2,1)S(1)} collective-permute-done((bf16[128,2560]{1,0:T(8,128)(2,1)S(1)}, bf16[128,2560]{1,0:T(8,128)(2,1)S(1)}, u32[]{:S(2)}, u32[]{:S(2)}) %collective-permute-start.10) | collective-permute-done | bytes 655392 | tf_op jit(solution)/shard_map/ppermute | solution.py:86
  508.1 10.1 collective-permute-start.13
  520.0 17.0 collective-permute-done.12
  538.9 17.0 collective-permute-done.14
  562.5 12.2 fusion.75
  574.7 64.3 %all-gather.18.cloned.1.call-done = bf16[2560,2048]{1,0:T(8,128)(2,1)} async-done(((bf16[2560,128]{1,0:T(8,128)(2,1)}), bf16[2560,2048]{1,0:T(8,128)(2,1)}) %all-gather.18.cloned.1.call-update) | async-done | bytes 10485776 | tf_op jit(solution)/shard_map/all_gather | solution.py:187
  639.0 12.3 fusion.76
  651.4 16.7 multiply_convert_fusion.1
  669.8 11.2 fusion.77
  681.0 46.6 %all-gather.20.cloned.1.call-done = bf16[2048,2560]{1,0:T(8,128)(2,1)} async-done(((bf16[128,2560]{1,0:T(8,128)(2,1)}), bf16[2048,2560]{1,0:T(8,128)(2,1)}) %all-gather.20.cloned.1.call-update) | async-done | bytes 10485776 | tf_op jit(solution)/shard_map/all_gather | solution.py:217
  727.6 12.9 add_convert_fusion
  740.6 72.6 %all-reduce.12.cloned.1.call-done = bf16[640,2048]{1,0:T(8,128)(2,1)} async-done(((bf16[640,2048]{1,0:T(8,128)(2,1)}), bf16[640,2048]{1,0:T(8,128)(2,1)}) %all-reduce.12.cloned.1.call-update) | async-done | bytes 2621456 | tf_op jit(solution)/shard_map/psum | solution.py:56
  813.2 4.7 fusion.43
  818.1 6.8 convolution_convert_fusion.3
  827.9 208.5 %while.35 = (s32[]{:T(128)}, f32[1536,320]{0,1:T(8,128)}, f32[1536,320]{0,1:T(8,128)}, f32[10,640,64]{1,2,0:T(8,128)}, s32[10]{0:T(128)S(1)}, /*index=5*/s32[]{:...) while((s32[]{:T(128)}, f32[1536,320]{0,1:T(8,128)}, ...), condition=%wide.region_14.15_spmd.clone.clone, body=%wide.region_12.14_spmd.clone.sunk.clone | while | flops 643104128 | bytes 48826372 | solution.py:253
  836.4 4.7 multiply_reduce_fusion.10
  857.2 4.7 multiply_reduce_fusion.10
  878.1 4.7 multiply_reduce_fusion.10
  898.9 4.7 multiply_reduce_fusion.10
  919.7 4.7 multiply_reduce_fusion.10
  940.6 4.7 multiply_reduce_fusion.10
  961.5 4.7 multiply_reduce_fusion.10
  982.3 4.7 multiply_reduce_fusion.10
  1003.2 4.7 multiply_reduce_fusion.10
  1024.0 4.7 multiply_reduce_fusion.10
  1040.4 12.0 convolution_convert_fusion.1
  1067.9 34.9 %reduce-scatter.30.cloned.1.call-done = bf16[128,320]{1,0:T(8,128)(2,1)} async-done(((bf16[1024,320]{1,0:T(8,128)(2,1)}), bf16[128,320]{1,0:T(8,128)(2,1)}) %reduce-scatter.30.cloned.1.call-update) | async-done | bytes 81936
  1104.7 63.8 %reduce-scatter.28.cloned.1.call-done = bf16[128,320]{1,0:T(8,128)(2,1)} async-done(((bf16[1024,320]{1,0:T(8,128)(2,1)}), bf16[128,320]{1,0:T(8,128)(2,1)}) %reduce-scatter.28.cloned.1.call-update) | async-done | bytes 81936
  1171.5 8.2 fusion.53
  1180.8 6.6 fusion.79
  1187.7 132.1 %all-reduce.14.cloned.1.call-done = (bf16[640,2048]{1,0:T(8,128)(2,1)}, bf16[640,5,64]{0,2,1:T(8,128)(2,1)}, bf16[640,2048]{1,0:T(8,128)(2,1)}, bf16[640,320]{0,1:T(8,128)(2,1)}) async-done(((bf16[640,2048]{1,0:T(8,128)(2,1)}, bf16[640,5,64]{0,2,1:T(8,128)(2,1)}, bf16[640,2048]{1,0:T(8,128)(2,1)}, bf16[640,320]{0,1:T(8,128)(2,1)}), (bf16[640,2048]{1,0:T(8,128)(2,1)}, bf16[640,5,64]{0,2,1:T(8,128)(2,1)}, ...) | async-done | bytes 6062096 | tf_op jit(solution)/shard_map/psum | solution.py:56
  1326.4 4.5 fusion.84
  1331.0 15.2 fusion.80
  1346.3 14.9 fusion.81
  1361.5 14.8 fusion.82
  1376.3 5.1 psum.84
  1388.8 5.9 fusion.46
  1399.2 60.7 %all-reduce.4 = (f32[2048]{0:T(1024)}, f32[64]{0:T(128)}, f32[64]{0:T(128)}, f32[2048]{0:T(1024)}) all-reduce(f32[2048]{0:T(1024)S(1)} %get-tuple-element.423, bf16[64]{0:T(256)(128)(2,1)S(1)} %psum.84, f32[64]{0:T(128)S(1)} %get-tuple-element.427, f32[2048]{0:T(1024)S(1)} %copy-done.49), channel_id=1, replica_groups=mesh['dp'=2,'ctx'=8,'tp'=2] {'dp','ctx'}, use_global_device_ids=true, to_apply=%region_24.25 | all-reduce | flops 4224 | bytes 33664 | tf_op jit(solution)/shard_map/psum | solution.py:301
  1459.9 26.3 %reduce-scatter.14.cloned.1.call-done = f32[128,640]{1,0:T(8,128)} async-done(((f32[2048,640]{1,0:T(8,128)}), f32[128,640]{1,0:T(8,128)}) %reduce-scatter.14.cloned.1.call-update) | async-done | bytes 327696 | tf_op jit(solution)/shard_map/reduce_scatter | solution.py:291
  1486.2 67.5 %reduce-scatter.16.cloned.1.call-done = f32[128,320]{0,1:T(8,128)} async-done(((f32[2048,320]{0,1:T(8,128)}), f32[128,320]{0,1:T(8,128)}) %reduce-scatter.16.cloned.1.call-update) | async-done | bytes 163856 | tf_op jit(solution)/shard_map/reduce_scatter | solution.py:292
  1553.7 67.6 %reduce-scatter.18.cloned.1.call-done = f32[128,320]{0,1:T(8,128)} async-done(((f32[2048,320]{0,1:T(8,128)}), f32[128,320]{0,1:T(8,128)}) %reduce-scatter.18.cloned.1.call-update) | async-done | bytes 163856 | tf_op jit(solution)/shard_map/reduce_scatter | solution.py:293
  1621.3 214.9 %reduce-scatter.22.cloned.1.call-done = f32[128,2560]{1,0:T(8,128)} async-done(((f32[2048,2560]{1,0:T(8,128)}), f32[128,2560]{1,0:T(8,128)}) %reduce-scatter.22.cloned.1.call-update) | async-done | bytes 1310736 | tf_op jit(solution)/shard_map/reduce_scatter | solution.py:294
  1836.3 215.1 %reduce-scatter.24.cloned.1.call-done = f32[128,2560]{1,0:T(8,128)} async-done(((f32[2048,2560]{1,0:T(8,128)}), f32[128,2560]{1,0:T(8,128)}) %reduce-scatter.24.cloned.1.call-update) | async-done | bytes 1310736 | tf_op jit(solution)/shard_map/reduce_scatter | solution.py:295
  2051.3 215.3 %reduce-scatter.26.cloned.1.call-done = f32[2560,128]{1,0:T(8,128)} async-done(((f32[2560,2048]{1,0:T(8,128)}), f32[2560,128]{1,0:T(8,128)}) %reduce-scatter.26.cloned.1.call-update) | async-done | bytes 1310736 | tf_op jit(solution)/shard_map/reduce_scatter | solution.py:299
  (461 shorter events, 360.0 us)
Async XLA Ops:
  7.2 8.1 copy-start.11
  7.2 8.1 copy-start.2
  7.2 6.7 copy-start.54
  7.2 6.8 copy-start.56
  7.2 8.0 copy-start.57
  7.2 43.4 %all-gather.10.cloned.1.call-start = ((), (), s32[]{:S(2)}) async-start(), calls=%async_computation.10 | async-start | bytes 1392640 | tf_op jit(solution)/shard_map/all_gather | solution.py:138
  8.0 81.9 %all-gather.12.cloned.1.call-start = ((), (), s32[]{:S(2)}) async-start(), calls=%async_computation.11 | async-start | bytes 1392640 | tf_op jit(solution)/shard_map/all_gather | solution.py:139
  8.7 153.1 %all-gather.8.cloned.1.call-start = ((), (), s32[]{:S(2)}) async-start(), calls=%async_computation.9 | async-start | bytes 2785280 | tf_op jit(solution)/shard_map/all_gather | solution.py:137
  9.5 285.6 %all-gather.14.cloned.1.call-start = ((), (), s32[]{:S(2)}) async-start(), calls=%async_computation.12 | async-start | bytes 2785280 | tf_op jit(solution)/shard_map/all_gather | solution.py:186
  10.0 546.7 %all-reduce.10.cloned.1.call-start = ((), (), s32[]{:S(2)}) async-start(), calls=%async_computation.13 | async-start | bytes 5242880 | tf_op jit(solution)/shard_map/psum | solution.py:56
  14.0 40.0 %copy-start.47 = (f32[640]{0:T(1024)}, f32[640]{0:T(1024)S(1)}, u32[]{:S(2)}) copy-start(f32[640]{0:T(1024)S(1)} %fusion.65) | copy-start | bytes 7684
  14.0 40.0 %copy-start.43 = (f32[2048]{0:T(1024)}, f32[2048]{0:T(1024)S(1)}, u32[]{:S(2)}) copy-start(f32[2048]{0:T(1024)S(1)} %convert_element_type.139) | copy-start | bytes 24580
  14.0 40.1 %copy-start.50 = (f32[64]{0:T(128)}, f32[64]{0:T(128)S(1)}, u32[]{:S(2)}) copy-start(f32[64]{0:T(128)S(1)} %convert_element_type.144) | copy-start | bytes 772
  15.1 152.6 %copy-start.20 = (f32[640,64]{0,1:T(8,128)}, f32[640,64]{0,1:T(8,128)S(1)}, u32[]{:S(2)}) copy-start(f32[640,64]{0,1:T(8,128)S(1)} %get-tuple-element.514) | copy-start | bytes 491524
  15.1 152.7 %copy-start.15 = (f32[640,64]{0,1:T(8,128)}, f32[640,64]{0,1:T(8,128)S(1)}, u32[]{:S(2)}) copy-start(f32[640,64]{0,1:T(8,128)S(1)} %get-tuple-element.513) | copy-start | bytes 491524
  15.2 151.6 %copy-start.52 = (f32[64]{0:T(128)}, f32[64]{0:T(128)S(1)}, u32[]{:S(2)}) copy-start(f32[64]{0:T(128)S(1)} %convert_element_type.141) | copy-start | bytes 772
  55.7 68.6 %copy-start.30 = (bf16[512,320]{0,1:T(8,128)(2,1)S(1)}, bf16[512,320]{0,1:T(8,128)(2,1)}, u32[]{:S(2)}) copy-start(bf16[512,320]{0,1:T(8,128)(2,1)} %slice.75) | copy-start | bytes 983044
  300.9 8.6 copy-start.55
  300.9 261.7 %all-gather.16.cloned.1.call-start = ((), (), s32[]{:S(2)}) async-start(), calls=%async_computation.14 | async-start | bytes 11141120 | tf_op jit(solution)/shard_map/all_gather | solution.py:196
  301.5 337.6 %all-gather.18.cloned.1.call-start = ((), (), s32[]{:S(2)}) async-start(), calls=%async_computation.15 | async-start | bytes 11141120 | tf_op jit(solution)/shard_map/all_gather | solution.py:187
  302.2 425.4 %all-gather.20.cloned.1.call-start = ((), (), s32[]{:S(2)}) async-start(), calls=%async_computation.16 | async-start | bytes 11141120 | tf_op jit(solution)/shard_map/all_gather | solution.py:217
  303.0 510.3 %all-reduce.12.cloned.1.call-start = ((), (), s32[]{:S(2)}) async-start(), calls=%async_computation.17 | async-start | bytes 5242880 | tf_op jit(solution)/shard_map/psum | solution.py:56
  303.0 20.5 collective-permute-start
  303.1 24.0 %collective-permute-start.1 = (bf16[128,2560]{1,0:T(8,128)(2,1)}, bf16[128,2560]{1,0:T(8,128)(2,1)}, u32[]{:S(2)}, u32[]{:S(2)}) collective-permute-start(bf16[128,2560]{1,0:T(8,128)(2,1)} %param.32), channel_id=1, source_target_pairs={{0,30},{2,0},{4,2},{6,4},{8,6},{10,8},{12,10},{14,12},{16,14},{18,... | collective-permute-start | bytes 1966088 | tf_op jit(solution)/shard_map/ppermute | solution.py:93
  323.5 28.9 %collective-permute-start.2 = (bf16[128,2560]{1,0:T(8,128)(2,1)}, bf16[128,2560]{1,0:T(8,128)(2,1)S(1)}, u32[]{:S(2)}, u32[]{:S(2)}) collective-permute-start(bf16[128,2560]{1,0:T(8,128)(2,1)} %collective-permute-done), channel_id=1, source_target_pairs={{0,2},{2,4},{4,6},{6,8},{8,10},{10,12},{12,14},{14,16},{16,18},{18... | collective-permute-start | bytes 1966088 | tf_op jit(solution)/shard_map/ppermute | solution.py:86
  327.0 27.8 %collective-permute-start.3 = (bf16[128,2560]{1,0:T(8,128)(2,1)}, bf16[128,2560]{1,0:T(8,128)(2,1)S(1)}, u32[]{:S(2)}, u32[]{:S(2)}) collective-permute-start(bf16[128,2560]{1,0:T(8,128)(2,1)} %collective-permute-done.1), channel_id=1, source_target_pairs={{0,30},{2,0},{4,2},{6,4},{8,6},{10,8},{12,10},{14,12},{16,14},{18,... | collective-permute-start | bytes 1966088 | tf_op jit(solution)/shard_map/ppermute | solution.py:93
  352.4 29.7 %collective-permute-start.4 = (bf16[128,2560]{1,0:T(8,128)(2,1)S(1)}, bf16[128,2560]{1,0:T(8,128)(2,1)S(1)}, u32[]{:S(2)}, u32[]{:S(2)}) collective-permute-start(bf16[128,2560]{1,0:T(8,128)(2,1)S(1)} %collective-permute-done.2), channel_id=1, source_target_pairs={{0,2},{2,4},{4,6},{6,8},{8,10},{10,12},{12,14},{14,16},{16,18},{18... | collective-permute-start | bytes 1966088 | tf_op jit(solution)/shard_map/ppermute | solution.py:86
  354.8 30.0 %collective-permute-start.5 = (bf16[128,2560]{1,0:T(8,128)(2,1)S(1)}, bf16[128,2560]{1,0:T(8,128)(2,1)S(1)}, u32[]{:S(2)}, u32[]{:S(2)}) collective-permute-start(bf16[128,2560]{1,0:T(8,128)(2,1)S(1)} %collective-permute-done.3), channel_id=1, source_target_pairs={{0,30},{2,0},{4,2},{6,4},{8,6},{10,8},{12,10},{14,12},{16,14},{18,... | collective-permute-start | bytes 1966088 | tf_op jit(solution)/shard_map/ppermute | solution.py:93
  382.2 36.9 %collective-permute-start.6 = (bf16[128,2560]{1,0:T(8,128)(2,1)S(1)}, bf16[128,2560]{1,0:T(8,128)(2,1)S(1)}, u32[]{:S(2)}, u32[]{:S(2)}) collective-permute-start(bf16[128,2560]{1,0:T(8,128)(2,1)S(1)} %collective-permute-done.4), channel_id=1, source_target_pairs={{0,2},{2,4},{4,6},{6,8},{8,10},{10,12},{12,14},{14,16},{16,18},{18... | collective-permute-start | bytes 1966088 | tf_op jit(solution)/shard_map/ppermute | solution.py:86
  384.8 36.7 %collective-permute-start.7 = (bf16[128,2560]{1,0:T(8,128)(2,1)S(1)}, bf16[128,2560]{1,0:T(8,128)(2,1)S(1)}, u32[]{:S(2)}, u32[]{:S(2)}) collective-permute-start(bf16[128,2560]{1,0:T(8,128)(2,1)S(1)} %collective-permute-done.5), channel_id=1, source_target_pairs={{0,30},{2,0},{4,2},{6,4},{8,6},{10,8},{12,10},{14,12},{16,14},{18,... | collective-permute-start | bytes 1966088 | tf_op jit(solution)/shard_map/ppermute | solution.py:93
  419.1 44.6 %collective-permute-start.8 = (bf16[128,2560]{1,0:T(8,128)(2,1)S(1)}, bf16[128,2560]{1,0:T(8,128)(2,1)S(1)}, u32[]{:S(2)}, u32[]{:S(2)}) collective-permute-start(bf16[128,2560]{1,0:T(8,128)(2,1)S(1)} %collective-permute-done.6), channel_id=1, source_target_pairs={{0,2},{2,4},{4,6},{6,8},{8,10},{10,12},{12,14},{14,16},{16,18},{18... | collective-permute-start | bytes 1966088 | tf_op jit(solution)/shard_map/ppermute | solution.py:86
  421.6 44.6 %collective-permute-start.9 = (bf16[128,2560]{1,0:T(8,128)(2,1)S(1)}, bf16[128,2560]{1,0:T(8,128)(2,1)S(1)}, u32[]{:S(2)}, u32[]{:S(2)}) collective-permute-start(bf16[128,2560]{1,0:T(8,128)(2,1)S(1)} %collective-permute-done.7), channel_id=1, source_target_pairs={{0,30},{2,0},{4,2},{6,4},{8,6},{10,8},{12,10},{14,12},{16,14},{18,... | collective-permute-start | bytes 1966088 | tf_op jit(solution)/shard_map/ppermute | solution.py:93
  463.6 42.0 %collective-permute-start.10 = (bf16[128,2560]{1,0:T(8,128)(2,1)S(1)}, bf16[128,2560]{1,0:T(8,128)(2,1)S(1)}, u32[]{:S(2)}, u32[]{:S(2)}) collective-permute-start(bf16[128,2560]{1,0:T(8,128)(2,1)S(1)} %collective-permute-done.8), channel_id=1, source_target_pairs={{0,2},{2,4},{4,6},{6,8},{8,10},{10,12},{12,14},{14,16},{16,18},{18... | collective-permute-start | bytes 1966088 | tf_op jit(solution)/shard_map/ppermute | solution.py:86
  466.1 42.0 %collective-permute-start.11 = (bf16[128,2560]{1,0:T(8,128)(2,1)S(1)}, bf16[128,2560]{1,0:T(8,128)(2,1)S(1)}, u32[]{:S(2)}, u32[]{:S(2)}) collective-permute-start(bf16[128,2560]{1,0:T(8,128)(2,1)S(1)} %collective-permute-done.9), channel_id=1, source_target_pairs={{0,30},{2,0},{4,2},{6,4},{8,6},{10,8},{12,10},{14,12},{16,14},{18,... | collective-permute-start | bytes 1966088 | tf_op jit(solution)/shard_map/ppermute | solution.py:93
  505.6 31.4 %collective-permute-start.12 = (bf16[128,2560]{1,0:T(8,128)(2,1)S(1)}, bf16[128,2560]{1,0:T(8,128)(2,1)S(1)}, u32[]{:S(2)}, u32[]{:S(2)}) collective-permute-start(bf16[128,2560]{1,0:T(8,128)(2,1)S(1)} %collective-permute-done.10), channel_id=1, source_target_pairs={{0,2},{2,4},{4,6},{6,8},{8,10},{10,12},{12,14},{14,16},{16,18},{18... | collective-permute-start | bytes 1966088 | tf_op jit(solution)/shard_map/ppermute | solution.py:86
  508.1 29.9 %collective-permute-start.13 = (bf16[128,2560]{1,0:T(8,128)(2,1)S(1)}, bf16[128,2560]{1,0:T(8,128)(2,1)S(1)}, u32[]{:S(2)}, u32[]{:S(2)}) collective-permute-start(bf16[128,2560]{1,0:T(8,128)(2,1)S(1)} %collective-permute-done.11), channel_id=1, source_target_pairs={{0,30},{2,0},{4,2},{6,4},{8,6},{10,8},{12,10},{14,12},{16,14},{18,... | collective-permute-start | bytes 1966088 | tf_op jit(solution)/shard_map/ppermute | solution.py:93
  537.0 18.9 collective-permute-start.14
  639.0 12.3 copy-start.27
  740.6 362.3 %reduce-scatter.30.cloned.1.call-start = ((), (), s32[]{:S(2)}) async-start(), calls=%async_computation.26 | async-start | bytes 884736
  813.2 4.8 copy-start.4
  813.2 4.8 copy-start.13
  813.2 4.9 copy-start.24
  836.3 4.7 copy-start
  878.0 4.7 copy-start
  898.9 4.7 copy-start
  919.7 4.7 copy-start
  982.3 4.7 copy-start
  1040.3 128.2 %reduce-scatter.28.cloned.1.call-start = ((), (), s32[]{:S(2)}) async-start(), calls=%async_computation.25 | async-start | bytes 884736
  1040.4 12.0 copy-start.12
  1058.8 261.0 %all-reduce.14.cloned.1.call-start = ((), (), s32[]{:S(2)}) async-start(), calls=%async_computation.27 | async-start | bytes 12124160 | tf_op jit(solution)/shard_map/psum | solution.py:56
  1064.2 39.7 %slice-start = ((bf16[1536,320]{0,1:T(8,128)(2,1)}), bf16[512,320]{0,1:T(8,128)(2,1)S(1)}, s32[]{:S(2)}) async-start(bf16[1536,320]{0,1:T(8,128)(2,1)} %copy-done.22), calls=%async_computation.28 | async-start | bytes 655360 | tf_op jit(solution)/shard_map/slice | solution.py:268
  1064.2 105.3 %slice-start.1 = ((bf16[1536,320]{0,1:T(8,128)(2,1)}), bf16[512,320]{0,1:T(8,128)(2,1)S(1)}, s32[]{:S(2)}) async-start(bf16[1536,320]{0,1:T(8,128)(2,1)} %copy-done.23), calls=%async_computation.29 | async-start | bytes 655360 | tf_op jit(solution)/shard_map/slice | solution.py:267
  1170.4 289.6 %reduce-scatter.20.cloned.1.call-start = ((), (), s32[]{:S(2)}) async-start(), calls=%async_computation.21 | async-start | bytes 5570560 | tf_op jit(solution)/shard_map/reduce_scatter | solution.py:298
  1179.7 306.5 %reduce-scatter.14.cloned.1.call-start = ((), (), s32[]{:S(2)}) async-start(), calls=%async_computation.18 | async-start | bytes 5570560 | tf_op jit(solution)/shard_map/reduce_scatter | solution.py:291
  1187.4 133.7 %copy-start.10 = (f32[640,320]{0,1:T(8,128)S(1)}, f32[640,320]{0,1:T(8,128)}, u32[]{:S(2)}) copy-start(f32[640,320]{0,1:T(8,128)} %copy-done.9) | copy-start | bytes 2457604
  1187.4 133.7 %copy-start.38 = (f32[640,5]{0,1:T(8,128)S(1)}, f32[640,5]{0,1:T(8,128)}, u32[]{:S(2)}) copy-start(f32[640,5]{0,1:T(8,128)} %copy-done.37) | copy-start | bytes 38404
  1187.4 133.7 %copy-start.51 = (f32[64]{0:T(128)S(1)}, f32[64]{0:T(128)}, u32[]{:S(2)}) copy-start(f32[64]{0:T(128)} %copy-done.50) | copy-start | bytes 772
  1187.4 135.1 %copy-start.42 = (f32[640,5]{0,1:T(8,128)S(1)}, f32[640,5]{0,1:T(8,128)}, u32[]{:S(2)}) copy-start(f32[640,5]{0,1:T(8,128)} %copy-done.41) | copy-start | bytes 38404
  1187.4 366.3 %reduce-scatter.16.cloned.1.call-start = ((), (), s32[]{:S(2)}) async-start(), calls=%async_computation.19 | async-start | bytes 2785280 | tf_op jit(solution)/shard_map/reduce_scatter | solution.py:292
  1326.4 294.9 %reduce-scatter.18.cloned.1.call-start = ((), (), s32[]{:S(2)}) async-start(), calls=%async_computation.20 | async-start | bytes 2785280 | tf_op jit(solution)/shard_map/reduce_scatter | solution.py:293
  1330.9 505.3 %reduce-scatter.22.cloned.1.call-start = ((), (), s32[]{:S(2)}) async-start(), calls=%async_computation.22 | async-start | bytes 22282240 | tf_op jit(solution)/shard_map/reduce_scatter | solution.py:294
  1346.2 705.1 %reduce-scatter.24.cloned.1.call-start = ((), (), s32[]{:S(2)}) async-start(), calls=%async_computation.23 | async-start | bytes 22282240 | tf_op jit(solution)/shard_map/reduce_scatter | solution.py:295
  1361.2 905.5 %reduce-scatter.26.cloned.1.call-start = ((), (), s32[]{:S(2)}) async-start(), calls=%async_computation.24 | async-start | bytes 22282240 | tf_op jit(solution)/shard_map/reduce_scatter | solution.py:299
  1376.2 5.1 copy-start.19
  (52 other events, 127.5 us)
Sparse Core Ops, SparseCore 0:
  10.1 40.4 all-gather.9
  52.7 37.0 all-gather.11
  92.1 45.5 all-gather.7
  139.6 45.6 all-gather.13
  301.0 72.1 all-reduce.9
  375.5 155.8 all-gather.15
  533.7 105.3 all-gather.17
  641.5 86.0 all-gather.19
  740.7 72.4 all-reduce.11
  1040.4 62.4 reduce-scatter.29
  1107.1 61.3 reduce-scatter.27
  1171.6 148.2 all-reduce.13
  1324.8 78.4 reduce-scatter.19
  1408.0 78.1 reduce-scatter.13
  1490.9 62.8 reduce-scatter.15
  1558.4 62.8 reduce-scatter.17
  1626.4 209.8 reduce-scatter.21
  1841.3 209.9 reduce-scatter.23
  2056.6 209.9 reduce-scatter.25
